TPU v7x, 128 devices: a whole 4x4x4 slice. The times are simulated.
128 devices in a mesh: row: 8 (over y_lo, z), col: 16 (over x, y_hi, core).
Axes of the slice: x: 4, y: 4 (y_hi: 2, y_lo: 2; y = y_hi * 2 + y_lo), z: 4, core: 2. Of those that a mesh axis runs over, the one named last changes fastest.
Arguments:
- inverse: float32 [16384, 16384], P('row', 'col'), may hold values from -0.0625 to 0.0625
- pattern: int32 [128, 128], P('row', 'col'), may hold values 0 or 1
- factor_first: float32 [16384, 256], P('col'), may hold values from -1.5 to 1.5
- factor_second: float32 [16384, 256], P('col'), may hold values from -1.5 to 1.5
- rows_first: int32 [64], replicated, may hold values from 0 to 127, as said below
- rows_second: int32 [64], replicated, may hold values from 0 to 127, as said below
- coupling: float32 [256, 256], replicated, may hold values from -0.375 to 0.375
- diag_first: float32 [256, 256], replicated, may hold values from -6 to 6
- diag_second: float32 [256, 256], replicated, may hold values from -6 to 6
Outputs:
- panel_one: float32 [16384, 256], P(('row', 'col'))
- panel_two: float32 [16384, 256], P(('row', 'col'))
- block_one: float32 [256, 256], replicated
- block_cross: float32 [256, 256], replicated
- block_two: float32 [256, 256], replicated
Inputs may be any that keep to these rules, and one draw needn't show every extreme that they name: `rows_first`: 64 distinct block indices in increasing order; the first block, the block 64 and the last block are always among them. `rows_second`: 64 distinct block indices in increasing order; the first block, the block 64 and the last block are always among them.
All inputs are finite; a program needn't handle non-finite values. No bound on the sum of `pattern` on one device may be relied on, other than what follows from the above.
Results may differ from a plain program's by a relative error of at most 0.000071.
Values sent between devices are 32-bit elements; how exact they have to be, the bound alone decides.
A program may use at most 128 MiB of HBM per device.

v0:
```python
import jax
import jax.numpy as jnp
from jax import lax
from jax.sharding import PartitionSpec as P

BLK = 128


def member(block_ids, rows_list):
    hits = (block_ids[:, None] == rows_list[None, :]).astype(jnp.float32)
    return jnp.sum(hits, axis=1)


def per_device(
    inverse,
    pattern,
    factor_first,
    factor_second,
    rows_first,
    rows_second,
    coupling,
    diag_first,
    diag_second,
):
    high = lax.Precision.HIGHEST
    col_count = lax.axis_size("col")
    row_index = lax.axis_index("row")
    col_index = lax.axis_index("col")
    share_rows = factor_first.shape[0]
    local_rows, local_cols = inverse.shape
    quota_rows = local_rows // col_count
    masked = (
        inverse.reshape(local_rows // BLK, BLK, local_cols // BLK, BLK)
        * pattern.astype(jnp.float32)[:, None, :, None]
    ).reshape(local_rows, local_cols)
    share_ids = (col_index * share_rows + jnp.arange(share_rows, dtype=jnp.int32)) // BLK
    own_start = (row_index * col_count + col_index) * quota_rows
    own_ids = (own_start + jnp.arange(quota_rows, dtype=jnp.int32)) // BLK

    def fetch_rows(factor):
        gathered = lax.all_gather(factor, "col", axis=0, tiled=True)
        return lax.dynamic_slice_in_dim(gathered, own_start, quota_rows, 0)

    def panel_product(factor_kept):
        return lax.psum_scatter(
            jnp.dot(masked, factor_kept, precision=high), "col", scatter_dimension=0, tiled=True
        )

    x_one = factor_first * member(share_ids, rows_first)[:, None]
    x_two = factor_second * member(share_ids, rows_second)[:, None]
    panel_one = -panel_product(x_one)
    near_one = fetch_rows(factor_first)
    near_one = near_one * member(own_ids, rows_first)[:, None]
    first_total = lax.psum(jnp.dot(near_one.T, panel_one, precision=high), ("row", "col"))
    block_one = diag_first - first_total
    near_two = fetch_rows(factor_second)
    near_two = near_two * member(own_ids, rows_second)[:, None]
    panel_two = -(panel_product(x_two) + jnp.dot(panel_one, coupling, precision=high))
    cross_sum, quad_sum = lax.psum(
        (
            jnp.dot(panel_one.T, near_two, precision=high),
            jnp.dot(near_two.T, panel_two, precision=high),
        ),
        ("row", "col"),
    )
    block_cross = -(cross_sum + jnp.dot(block_one, coupling, precision=high))
    block_two = diag_second - quad_sum - jnp.dot(coupling.T, block_cross, precision=high)
    return (panel_one, panel_two, block_one, block_cross, block_two)


def solution(mesh):
    return jax.shard_map(
        per_device,
        mesh=mesh,
        in_specs=(
            P("row", "col"),
            P("row", "col"),
            P("col", None),
            P("col", None),
            P(),
            P(),
            P(),
            P(),
            P(),
        ),
        out_specs=(P(("row", "col"), None), P(("row", "col"), None), P(), P(), P()),
        check_vma=False,
    )
```

profile of v0, /device:TPU:1, one launch (start us, length us, event | category | flops | bytes accessed | tf_op | source)
XLA Modules:
  0.0 555.6 jit_solution(4285565588301605714)
XLA Ops:
  7.2 0.7 convert_element_type.15
  8.0 1.0 convert_reduce_fusion
  9.0 0.6 mul.52
  9.6 3.8 copy-done.1
  13.4 0.1 copy-done.2
  13.5 10.3 %fusion.1 = f32[2048,256]{1,0:T(8,128)} fusion(f32[2048,1024]{1,0:T(8,128)S(1)} %copy-done.2, f32[256,8,8,128]{3,2,1,0:T(8,128)S(1)} %bitcast.19, f32[1024,256]{1,0:T(8,128)} %param.11, f32[1024]{0:T(1024)S(1)} %get-tuple-element.6), kind=kOutput, calls=%fused_computation.2 | convolution fusion | flops 6444810240 | bytes 19927040 | tf_op jit(solution)/shard_map/dot_general | solution.py:46
  23.8 0.2 reduce-scatter.5.cloned.1.call-start
  24.1 12.9 %fusion = f32[2048,256]{1,0:T(8,128)} fusion(f32[2048,1024]{1,0:T(8,128)} %param.9, f32[256,8,8,128]{3,2,1,0:T(8,128)} %bitcast.20, f32[1024,256]{1,0:T(8,128)S(1)} %copy-done.3, f32[1024]{0:T(1024)S(1)} %get-tuple-element.5), kind=kOutput, calls=%fused_computation.1 | convolution fusion | flops 6444810240 | bytes 19927040 | tf_op jit(solution)/shard_map/dot_general | solution.py:46
  37.0 0.7 all-gather.5.cloned.1.call-update
  37.8 0.5 all-gather.3.cloned.1.call-update
  38.4 0.1 convert_reduce_fusion.2
  38.5 57.6 %reduce-scatter.3.cloned.1.call-done = f32[128,256]{1,0:T(8,128)} async-done(((f32[2048,256]{1,0:T(8,128)}), f32[128,256]{1,0:T(8,128)}) %reduce-scatter.3.cloned.1.call-update) | async-done | bytes 131088 | tf_op jit(solution)/shard_map/reduce_scatter | solution.py:45
  96.1 0.9 neg.9
  97.0 73.0 %reduce-scatter.5.cloned.1.call-done = f32[128,256]{1,0:T(8,128)} async-done(((f32[2048,256]{1,0:T(8,128)}), f32[128,256]{1,0:T(8,128)}) %reduce-scatter.5.cloned.1.call-update) | async-done | bytes 131088 | tf_op jit(solution)/shard_map/reduce_scatter | solution.py:45
  170.0 1.2 fusion.4
  171.2 112.4 %all-gather.5.cloned.1.call-done = f32[16384,256]{1,0:T(8,128)} async-done(((f32[1024,256]{1,0:T(8,128)}), f32[16384,256]{1,0:T(8,128)}) %all-gather.5.cloned.1.call-update) | async-done | bytes 16777232 | tf_op jit(solution)/shard_map/all_gather | solution.py:41
  283.5 2.1 fusion.13
  285.6 2.1 fusion.12
  287.7 105.6 %all-gather.3.cloned.1.call-done = f32[16384,256]{1,0:T(8,128)} async-done(((f32[1024,256]{1,0:T(8,128)}), f32[16384,256]{1,0:T(8,128)}) %all-gather.3.cloned.1.call-update) | async-done | bytes 16777232 | tf_op jit(solution)/shard_map/all_gather | solution.py:41
  393.3 2.1 fusion.9
  395.4 148.9 %all-reduce.3.cloned.1.call-done = (f32[256,256]{1,0:T(8,128)}, f32[256,256]{1,0:T(8,128)}, f32[256,256]{1,0:T(8,128)}) async-done(((f32[256,256]{1,0:T(8,128)}, f32[256,256]{1,0:T(8,128)}, f32[256,256]{1,0:T(8,128)}), (f32[256,256]{1,0:T(8,128)}, f32[256,256]{1,0:T(8,128)}, f32[256,256]{1,0:T(8,128)})) %all-reduce.3.cloned.1.call-update) | async-done | bytes 786448 | tf_op jit(solution)/shard_map/psum | solution.py:54
  544.3 1.0 sub.23
  545.3 1.4 fusion.3
  546.7 2.3 fusion.2
  (32 shorter events, 0.4 us)
Async XLA Ops:
  7.2 162.8 %copy-start = (f32[256,256]{1,0:T(8,128)S(1)}, f32[256,256]{1,0:T(8,128)}, u32[]{:S(2)}) copy-start(f32[256,256]{1,0:T(8,128)} %param.15) | copy-start | bytes 786436
  7.2 88.9 %reduce-scatter.3.cloned.1.call-start = ((), (), s32[]{:S(2)}) async-start(), calls=%async_computation.2 | async-start | bytes 2228224 | tf_op jit(solution)/shard_map/reduce_scatter | solution.py:45
  8.0 5.5 copy-start.2
  9.6 3.8 copy-start.1
  13.5 10.5 %copy-start.3 = (f32[1024,256]{1,0:T(8,128)S(1)}, f32[1024,256]{1,0:T(8,128)}, u32[]{:S(2)}) copy-start(f32[1024,256]{1,0:T(8,128)} %param.12) | copy-start | bytes 3145732
  23.8 146.2 %reduce-scatter.5.cloned.1.call-start = ((), (), s32[]{:S(2)}) async-start(), calls=%async_computation.3 | async-start | bytes 2228224 | tf_op jit(solution)/shard_map/reduce_scatter | solution.py:45
  24.0 14.3 %copy-start.10 = (s32[64]{0:T(128)S(1)}, s32[64]{0:T(128)}, u32[]{:S(2)}) copy-start(s32[64]{0:T(128)} %param.14) | copy-start | bytes 772
  24.0 14.3 %copy-start.11 = (s32[64]{0:T(128)S(1)}, s32[64]{0:T(128)}, u32[]{:S(2)}) copy-start(s32[64]{0:T(128)} %param.13) | copy-start | bytes 772
  24.1 520.2 %copy-start.8 = (f32[256,256]{1,0:T(8,128)S(1)}, f32[256,256]{1,0:T(8,128)}, u32[]{:S(2)}) copy-start(f32[256,256]{1,0:T(8,128)} %param.16) | copy-start | bytes 786436
  36.9 509.8 %copy-start.9 = (f32[256,256]{1,0:T(8,128)S(1)}, f32[256,256]{1,0:T(8,128)}, u32[]{:S(2)}) copy-start(f32[256,256]{1,0:T(8,128)} %param.17) | copy-start | bytes 786436
  37.0 246.6 %all-gather.5.cloned.1.call-start = ((), (), s32[]{:S(2)}) async-start(), calls=%async_computation.5 | async-start | bytes 17825792 | tf_op jit(solution)/shard_map/all_gather | solution.py:41
  37.7 355.5 %all-gather.3.cloned.1.call-start = ((), (), s32[]{:S(2)}) async-start(), calls=%async_computation.4 | async-start | bytes 17825792 | tf_op jit(solution)/shard_map/all_gather | solution.py:41
  38.3 506.0 %all-reduce.3.cloned.1.call-start = ((), (), s32[]{:S(2)}) async-start(), calls=%async_computation.6 | async-start | bytes 1572864 | tf_op jit(solution)/shard_map/psum | solution.py:54
  97.0 452.1 %copy-start.4 = (f32[128,256]{1,0:T(8,128)}, f32[128,256]{1,0:T(8,128)S(1)}, u32[]{:S(2)}) copy-start(f32[128,256]{1,0:T(8,128)S(1)} %neg.9) | copy-start | bytes 393220
  171.2 377.9 %copy-start.7 = (f32[128,256]{1,0:T(8,128)}, f32[128,256]{1,0:T(8,128)S(1)}, u32[]{:S(2)}) copy-start(f32[128,256]{1,0:T(8,128)S(1)} %fusion.4) | copy-start | bytes 393220
  545.2 3.8 copy-start.5
  546.7 2.4 copy-start.6
Sparse Core Ops, SparseCore 0:
  23.9 72.0 reduce-scatter.2
  100.0 69.9 reduce-scatter.4
  172.4 111.1 all-gather.4
  285.8 107.4 all-gather.2
  398.7 145.5 all-reduce.2
where the time goes:
time: 556 us
  waiting for transfers between devices  499 us (90%)
  matrix products  34.3 us (6%)
  between operations  14 us (3%)
    all_gather x2, waiting for transfers between devices, fetch_rows(): gathered = lax.all_gather(factor, 'col', axis=0, tiled=True)  218 us
    psum x1, waiting for transfers between devices, per_device(): lax.psum(jnp.dot(near_one.T, panel_one, precision=high), ('row', 'col'))  149 us
    reduce_scatter x2, waiting for transfers between devices, panel_product(): lax.psum_scatter(jnp.dot(masked, factor_kept, precision=high), 'col', sca...  131 us
    dot_general x2, matrix products, panel_product(): jnp.dot(masked, factor_kept, precision=high)  23.1 us
  transfers between devices with their start and end apart: 5, of which 5 were waited for; matrix products, arithmetic and copies ran while one was open for 3% of the time, Pallas kernels for 0%

commit v1 on v0

v1 whole, which is shorter than its diff:
```python
import functools

import jax
import jax.numpy as jnp
from jax import lax
from jax.experimental import pallas as pl
from jax.experimental.pallas import tpu as pltpu
from jax.sharding import PartitionSpec as P

MESH = pl.DeviceIdType.MESH
F32 = jnp.float32
BF16 = jnp.bfloat16
BLK = 128
W = 256
XR = 72
NSTEP = 8

CORE = 0
NEAR = CORE + 8
LEG1 = NEAR + 2
LEG2 = LEG1 + 4
YLEG = LEG2 + 8
YF = YLEG + 1
YLEG1 = YF + 4
YLEG2 = YLEG1 + 2
GC = YLEG2 + 4
R1 = GC + 3
R2 = R1 + 48
R3 = R2 + 12
GF = R3 + 48
NMSG = GF + 3
ROUNDS = 3


def split(a):
    hi = a.astype(BF16)
    return hi, (a - hi.astype(F32)).astype(BF16)


def dot3(ah, al, bh, bl, dims=(((1,), (0,)), ((), ()))):
    d = functools.partial(lax.dot_general, dimension_numbers=dims, preferred_element_type=F32)
    return d(ah, bh) + d(al, bh) + d(ah, bl)


def kernel(
    inv_ref, pat_ref, f1_ref, f2_ref, rows1_ref, rows2_ref, coup_ref, d1_ref, d2_ref,
    p1_out, p2_out, b1_out, bc_out, b2_out,
    a, fac, xh, xl, own, give, got, near, nth, ntl, l1, r2, ry, yf, yl1, yr2,
    g, gc, r1, zs, res,
    ssem, rsem, lsem, asem, round_sem,
):
    row, col = lax.axis_index("row"), lax.axis_index("col")
    core = lax.rem(col, 2)
    pos = {"x": col // 4, "y": lax.rem(col // 2, 2) * 2 + row // 4, "z": lax.rem(row, 4)}
    other = 1 - core
    yh = lax.rem(col // 2, 2)

    def device(x, y, z, c):
        return (lax.rem(y, 2) * 4 + z, x * 4 + (y // 2) * 2 + c)

    def at(x=0, y=0, z=0, flip=False):
        return device(
            lax.rem(pos["x"] + x, 4), lax.rem(pos["y"] + y, 4), lax.rem(pos["z"] + z, 4),
            other if flip else core,
        )

    def send(src, dst, k, dev):
        pltpu.make_async_remote_copy(
            src, dst, ssem.at[k], rsem.at[k], device_id=dev, device_id_type=MESH
        ).start()

    me = at()

    def arrived(dst, k):
        pltpu.make_async_remote_copy(
            dst, dst, ssem.at[k], rsem.at[k], device_id=me, device_id_type=MESH
        ).wait_recv()

    def sent(src, k):
        pltpu.make_async_remote_copy(
            src, src, ssem.at[k], rsem.at[k], device_id=me, device_id_type=MESH
        ).wait_send()

    neighbours = [at(x=1), at(x=3), at(y=1), at(y=3), at(z=1), at(z=3)]
    x_up, x_down, y_two, mate = at(x=1), at(x=3), at(y=2), at(flip=True)

    y_lo, z = row // 4, lax.rem(row, 4)
    home = 2 * y_lo + z // 2
    src_z = lax.rem(pos["x"] + 4 - home + z + 1, 4)
    src_dev = device(home, lax.rem(z, 2) * 2 + yh, src_z, pos["x"] // 2)
    to_z = 2 * lax.rem(pos["x"], 2) + yh
    to_x = lax.rem(z + 8 - 1 - to_z + pos["x"], 4)
    to_ylo = pos["x"] // 2
    to_yh = y_lo
    serves = (core == to_x // 2).astype(jnp.int32)

    barrier = pltpu.get_barrier_semaphore()
    for dev in [*neighbours, y_two, mate, src_dev]:
        pl.semaphore_signal(barrier, inc=1, device_id=dev, device_id_type=MESH)

    loads = [
        pltpu.make_async_copy(f1_ref, fac.at[0], lsem.at[0]),
        pltpu.make_async_copy(f2_ref, fac.at[1], lsem.at[1]),
    ]
    for copy in loads:
        copy.start()

    def place(s):
        k = s // 2
        dx = jnp.where(k == 0, 2, jnp.where(k == 1, 1, jnp.where(k == 2, 3, 0)))
        tx = lax.rem(pos["x"] + dx, 4)
        tyh = lax.rem(yh + 1 - lax.rem(s, 2), 2)
        return tx * 2 + tyh

    def load_a(s):
        return pltpu.make_async_copy(
            inv_ref.at[pl.ds(pl.multiple_of(place(s) * 256, 256), 256)], a.at[s], asem.at[s]
        )

    for s in range(NSTEP):
        load_a(s).start()

    def member(rows_ref, first, count):
        ids = lax.broadcasted_iota(jnp.int32, (8, 64), 0) + first
        hits = (ids == rows_ref[...].reshape(1, 64)).astype(F32)
        return jnp.sum(hits, axis=1, keepdims=True)[:count]

    pl.semaphore_wait(barrier, 8 + 2 * serves)

    for copy in loads:
        copy.wait()

    @pl.when(serves == 1)
    def _():
        for c in range(2):
            block = lax.rem(to_x, 2) * 4 + to_yh * 2 + c
            rows = pl.ds(pl.multiple_of(block * BLK, BLK), BLK)
            pltpu.make_async_remote_copy(
                fac.at[:, rows], near, ssem.at[NEAR + c], rsem.at[NEAR],
                device_id=device(to_x, to_yh * 2 + to_ylo, to_z, c), device_id_type=MESH,
            ).start()

    for p, rows_ref in enumerate((rows1_ref, rows2_ref)):
        keep = member(rows_ref, col * 8, 8)
        for j in range(8):
            rows = slice(j * BLK, (j + 1) * BLK)
            hi, lo = split(fac[p, rows, :] * keep[j : j + 1, :])
            xh[rows, p * W : (p + 1) * W] = hi
            xl[rows, p * W : (p + 1) * W] = lo

    for dev in neighbours:
        pl.semaphore_signal(round_sem.at[0], inc=1, device_id=dev, device_id_type=MESH)

    def compute(s):
        load_a(s).wait()
        base = place(s) * 2
        parts = []
        for half in (other, core):
            r0 = pl.multiple_of(half * BLK, BLK)
            parts.append(
                jnp.concatenate(
                    [
                        a[s, pl.ds(r0, BLK), j * BLK : (j + 1) * BLK]
                        * pat_ref[base + half, j].astype(F32)
                        for j in range(8)
                    ],
                    axis=1,
                )
            )
        ah, al = split(jnp.concatenate(parts, axis=0))
        out = dot3(ah, al, xh[...], xl[...])
        for p in range(2):
            give[s, p] = out[:BLK, p * W : (p + 1) * W]
            own[s, p] = out[BLK:, p * W : (p + 1) * W]
        send(give.at[s], got.at[s], CORE + s, mate)

    lo_rows, hi_rows = pl.ds(0, XR), pl.ds(XR, BLK - XR)

    def fold(s):
        arrived(got.at[s], CORE + s)
        own[s] += got[s]

    def after(s):
        k, w = s // 2, s % 2
        if k == 0:
            send(own.at[s, 0, lo_rows], l1.at[w, 0], LEG1 + 2 * w, x_up)
            send(own.at[s, 1, lo_rows], l1.at[w, 1], LEG1 + 2 * w + 1, x_down)
        elif k == 1:
            send(own.at[s, 1, lo_rows], r2.at[w, 0, 1], LEG2 + 4 * w + 1, x_up)
        elif k == 2:
            send(own.at[s, 0, lo_rows], r2.at[w, 1, 0], LEG2 + 4 * w + 2, x_down)
        if w == 0:
            send(own.at[s, :, hi_rows], yf.at[k], YF + k, y_two)

    def relay(w):
        for d, s, dev in ((0, 2 + w, x_up), (1, 4 + w, x_down)):
            arrived(l1.at[w, d], LEG1 + 2 * w + d)
            own[s, d, :XR] += l1[w, d]
            send(own.at[s, d, lo_rows], r2.at[w, d, d], LEG2 + 4 * w + 2 * d + d, dev)

    def fold_y(k):
        arrived(yf.at[k], YF + k)
        own[2 * k + 1, :, XR:] += yf[k]

    def step(s, carry):
        compute(s)
        for t in range(NSTEP - 1):

            @pl.when(s == t + 1)
            def _(t=t):
                fold(t)
                after(t)
                if t == 4:
                    relay(0)
                if t == 6:
                    relay(1)

            if 1 <= t <= ROUNDS:

                @pl.when(s == t + 1)
                def _(t=t):
                    pl.semaphore_wait(round_sem.at[t - 1], 6)
                    if t < ROUNDS:
                        for dev in neighbours:
                            pl.semaphore_signal(
                                round_sem.at[t], inc=1, device_id=dev, device_id_type=MESH
                            )

        return carry

    lax.fori_loop(0, NSTEP, step, 0)
    fold(7)

    fold_y(0)
    send(own.at[1, 0, hi_rows], yl1.at[0], YLEG1, x_up)
    send(own.at[1, 1, hi_rows], yl1.at[1], YLEG1 + 1, x_down)

    small = [
        pltpu.make_async_copy(coup_ref, res.at[3], lsem.at[0]),
        pltpu.make_async_copy(d1_ref, res.at[4], lsem.at[1]),
        pltpu.make_async_copy(d2_ref, res.at[5], lsem.at[2]),
    ]
    for copy in small:
        copy.start()
    arrived(near, NEAR)
    own_id = row * 16 + col
    for p, rows_ref in enumerate((rows1_ref, rows2_ref)):
        keep = member(rows_ref, own_id, 1)
        hi, lo = split((near[p] * keep).T)
        nth[p], ntl[p] = hi, lo
    for copy in small:
        copy.wait()

    fold_y(1)
    send(own.at[3, 1, hi_rows], yr2.at[0, 1], YLEG2 + 1, x_up)
    fold_y(2)
    send(own.at[5, 0, hi_rows], yr2.at[1, 0], YLEG2 + 2, x_down)

    for d in range(2):
        for p in range(2):
            arrived(r2.at[0, d, p], LEG2 + 2 * d + p)
    own[6, :, :XR] += r2[0, 0] + r2[0, 1]
    send(own.at[6, :, lo_rows], ry, YLEG, y_two)

    for d, s, dev in ((0, 3, x_up), (1, 5, x_down)):
        arrived(yl1.at[d], YLEG1 + d)
        own[s, d, XR:] += yl1[d]
        send(own.at[s, d, hi_rows], yr2.at[d, d], YLEG2 + 2 * d + d, dev)
    fold_y(3)

    for d in range(2):
        for p in range(2):
            arrived(r2.at[1, d, p], LEG2 + 4 + 2 * d + p)
    own[7, :, :XR] += r2[1, 0] + r2[1, 1]
    for d in range(2):
        for p in range(2):
            arrived(yr2.at[d, p], YLEG2 + 2 * d + p)
    own[7, :, XR:] += yr2[0] + yr2[1]
    arrived(ry, YLEG)
    own[7, :, :XR] += ry[...]

    m1, m2 = own[7, 0], own[7, 1]
    m1h, m1l = split(m1)
    ch, cl = split(res[3])
    p2 = dot3(m1h, m1l, ch, cl) - m2
    p1_out[...] = -m1
    p2_out[...] = p2
    p2h, p2l = split(p2)
    m1t_h, m1t_l = split(m1.T)
    g[0] = dot3(nth[0], ntl[0], m1h, m1l)
    n2h, n2l = split(near[1] * member(rows2_ref, own_id, 1))
    g[1] = dot3(m1t_h, m1t_l, n2h, n2l)
    g[2] = dot3(nth[1], ntl[1], p2h, p2l)

    mine, theirs = pl.multiple_of(core * BLK, BLK), pl.multiple_of(other * BLK, BLK)
    half = pl.ds(mine, BLK)
    for m in range(3):
        send(g.at[m, pl.ds(theirs, BLK)], gc.at[m], GC + m, mate)

    planes = (("x", "y", "z"), ("y", "z", "x"), ("z", "x", "y"))

    def shifted(m, i, j, k):
        return at(**dict(zip(planes[m], (i, j, k))))

    def piece(m, i, j):
        u, v, _ = planes[m]
        index = lax.rem(pos[u] + i, 4) * 4 + lax.rem(pos[v] + j, 4)
        return pl.ds(pl.multiple_of(mine + index * 8, 8), 8)

    order = sorted(
        ((i, j) for i in range(4) for j in range(4) if (i, j) != (0, 0)),
        key=lambda q: -(min(q[0], 4 - q[0]) + min(q[1], 4 - q[1])),
    )
    for m in range(3):
        arrived(gc.at[m], GC + m)
        g[m, half] += gc[m]
        for i, j in order:
            q = i * 4 + j
            send(g.at[m, piece(m, i, j)], r1.at[m, q], R1 + 16 * m + q, shifted(m, i, j, 0))
    for m in range(3):
        total = g[m, piece(m, 0, 0)]
        for i, j in reversed(order):
            q = i * 4 + j
            arrived(r1.at[m, q], R1 + 16 * m + q)
            total += r1[m, q]
        slot = pos[planes[m][2]]
        zs[m, slot] = total
        for k in (2, 1, 3):
            send(zs.at[m, slot], zs.at[m, slot], R2 + 4 * m + k, shifted(m, 0, 0, k))
    for m in range(3):
        for k in (1, 3, 2):
            slot = lax.rem(pos[planes[m][2]] + 4 - k, 4)
            arrived(zs.at[m, slot], R2 + 4 * m + k)
        res[m, piece(m, 0, 0)] = (zs[m, 0] + zs[m, 1]) + (zs[m, 2] + zs[m, 3])
        for i, j in order:
            q = i * 4 + j
            send(res.at[m, piece(m, 0, 0)], res.at[m, piece(m, 0, 0)], R3 + 16 * m + q, shifted(m, i, j, 0))
    for m in range(3):
        for i, j in reversed(order):
            q = i * 4 + j
            arrived(res.at[m, piece(m, 4 - i, 4 - j)], R3 + 16 * m + q)
        send(res.at[m, half], res.at[m, half], GF + m, mate)
    for m in range(3):
        arrived(res.at[m, pl.ds(theirs, BLK)], GF + m)

    b1 = res[4] + res[0]
    b1h, b1l = split(b1)
    bc = res[1] - dot3(b1h, b1l, ch, cl)
    bch, bcl = split(bc)
    cth, ctl = split(res[3].T)
    b1_out[...] = b1
    bc_out[...] = bc
    b2_out[...] = res[5] - res[2] - dot3(cth, ctl, bch, bcl)

    for s in range(NSTEP):
        sent(give.at[s], CORE + s)

    @pl.when(serves == 1)
    def _():
        for c in range(2):
            sent(near, NEAR + c)

    for k in range(4):
        sent(l1.at[0, 0], LEG1 + k)
    for k in range(8):
        sent(l1.at[0, 0], LEG2 + k)
    sent(ry, YLEG)
    for k in range(4):
        sent(yf.at[0], YF + k)
        sent(yl1.at[0], YLEG2 + k)
    for k in range(2):
        sent(yl1.at[0], YLEG1 + k)
    for m in range(3):
        sent(gc.at[m], GC + m)
        sent(gc.at[m], GF + m)
        for q in range(1, 16):
            sent(r1.at[m, q], R1 + 16 * m + q)
            sent(r1.at[m, q], R3 + 16 * m + q)
        for k in range(1, 4):
            sent(r1.at[m, 0], R2 + 4 * m + k)


def per_device(inverse, pattern, first, second, rows1, rows2, coupling, diag1, diag2):
    any_, vmem, smem = (
        pl.BlockSpec(memory_space=pl.ANY),
        pl.BlockSpec(memory_space=pltpu.VMEM),
        pl.BlockSpec(memory_space=pltpu.SMEM),
    )
    V = pltpu.VMEM
    return pl.pallas_call(
        kernel,
        out_shape=[jax.ShapeDtypeStruct((BLK, W), F32)] * 2 + [jax.ShapeDtypeStruct((W, W), F32)] * 3,
        in_specs=[any_, smem, any_, any_, vmem, vmem, any_, any_, any_],
        out_specs=[vmem] * 5,
        scratch_shapes=[
            V((8, 256, 1024), F32),
            V((2, 1024, W), F32),
            V((1024, 2 * W), BF16),
            V((1024, 2 * W), BF16),
            V((8, 2, BLK, W), F32),
            V((8, 2, BLK, W), F32),
            V((8, 2, BLK, W), F32),
            V((2, BLK, W), F32),
            V((2, W, BLK), BF16),
            V((2, W, BLK), BF16),
            V((2, 2, XR, W), F32),
            V((2, 2, 2, XR, W), F32),
            V((2, XR, W), F32),
            V((4, 2, BLK - XR, W), F32),
            V((2, BLK - XR, W), F32),
            V((2, 2, BLK - XR, W), F32),
            V((3, W, W), F32),
            V((3, BLK, W), F32),
            V((3, 16, 8, W), F32),
            V((3, 4, 8, W), F32),
            V((6, W, W), F32),
            pltpu.SemaphoreType.DMA((NMSG,)),
            pltpu.SemaphoreType.DMA((NMSG,)),
            pltpu.SemaphoreType.DMA((3,)),
            pltpu.SemaphoreType.DMA((8,)),
            pltpu.SemaphoreType.REGULAR((ROUNDS,)),
        ],
        compiler_params=pltpu.CompilerParams(
            collective_id=0, has_side_effects=True, vmem_limit_bytes=62 * 2**20
        ),
    )(inverse, pattern, first, second, rows1, rows2, coupling, diag1, diag2)


def solution(mesh):
    return jax.shard_map(
        per_device,
        mesh=mesh,
        in_specs=(
            P("row", "col"), P("row", "col"), P("col", None), P("col", None),
            P(), P(), P(), P(), P(),
        ),
        out_specs=(P(("row", "col"), None), P(("row", "col"), None), P(), P(), P()),
        check_vma=False,
    )
```

time: 556 us -> 68 us (0.12)
  waiting for transfers between devices: 499 us -> 0 us
  Pallas kernels: 0 us -> 57.6 us
  matrix products: 34.3 us -> 0 us
  between operations: 14 us -> 0.64 us
    all_gather x2 -> x0, waiting for transfers between devices: 218 us -> none  [fetch_rows(): gathered = lax.all_gather(factor, 'col', axis=0, tiled=True)]
    psum x1 -> x0, waiting for transfers between devices: 149 us -> none  [per_device(): lax.psum(jnp.dot(near_one.T, panel_one, precision=high), ('row', 'col'))]
    reduce_scatter x2 -> x0, waiting for transfers between devices: 131 us -> none  [panel_product(): lax.psum_scatter(jnp.dot(masked, factor_kept, precision=high), 'col', sca...]
    pallas_call x0 -> x1, Pallas kernels: none -> 57.6 us  [per_device(): pl.pallas_call(kernel, out_shape=[jax.ShapeDtypeStruct((BLK, W), F32)] *...]
    dot_general x8 -> x0, matrix products: 34.3 us -> none  [the longest x2 23.1 us: panel_product(): jnp.dot(masked, factor_kept, precision=high)]
  transfers between devices with their start and end apart: 5 -> 0, of which waited for: 5 -> 0; matrix products, arithmetic and copies ran while one was open for 3% -> 0% of each run, Pallas kernels for 0% -> 0%
where the time goes in v1:
time: 68 us; the launch traced here: 67.7 us
  Pallas kernels  57.6 us (85%)
  local copies, waits for them, and re-layouts  9.5 us (14%)
    pallas_call x1, Pallas kernels, per_device(): pl.pallas_call(kernel, out_shape=[jax.ShapeDtypeStruct((BLK, W), F32)] *...  57.6 us
    unnamed x6, local copies, waits for them, and re-layouts  9.5 us

profile of v1, /device:TPU:1, one launch (start us, length us, event | category | flops | bytes accessed | tf_op | source)
XLA Modules:
  0.0 67.7 jit_solution(4126987732026318067)
XLA Ops:
  0.6 1.4 %copy.14.pat_ref = s32[16,8]{1,0:T(8,128)} copy(s32[16,8]{0,1:T(8,128)} %param.10) | data formatting | bytes 1024 | tf_op args[1]
  2.0 57.6 %shard_map.128 = (f32[128,256]{1,0:T(8,128)}, f32[128,256]{1,0:T(8,128)}, f32[256,256]{1,0:T(8,128)}, f32[256,256]{1,0:T(8,128)}, f32[256,256]{1,0:T(8,128)}) custom-call(f32[2048,1024]{1,0:T(8,128)} %inv_ref.1, s32[16,8]{1,0:T(8,128)} %copy.14.pat_ref, f32[1024,256]{1,0:T(8,128)} %f1_ref.1, f32[1024,256]{1,0:T(8,128)} %f2_ref.1, s32[64]{0:T(128)} %rows1_ref.1, ...), custom_call_target="tpu_custom_call" | custom-call | tf_op jit(solution)/shard_map/pallas_call | solution.py:390
  59.6 1.6 %copy.20 = f32[128,256]{1,0:T(8,128)} copy(f32[128,256]{1,0:T(8,128)} %get-tuple-element.10) | data formatting | bytes 262144
  61.1 1.6 %copy.21 = f32[128,256]{1,0:T(8,128)} copy(f32[128,256]{1,0:T(8,128)} %get-tuple-element.11) | data formatting | bytes 262144
  62.7 1.7 %copy.22 = f32[256,256]{1,0:T(8,128)} copy(f32[256,256]{1,0:T(8,128)} %get-tuple-element.12) | data formatting | bytes 524288
  64.4 1.7 %copy.23 = f32[256,256]{1,0:T(8,128)} copy(f32[256,256]{1,0:T(8,128)} %get-tuple-element.13) | data formatting | bytes 524288
  66.0 1.7 %copy.24 = f32[256,256]{1,0:T(8,128)} copy(f32[256,256]{1,0:T(8,128)} %get-tuple-element.14) | data formatting | bytes 524288

commit v2 on v1

v2 whole, which is shorter than its diff:
```python
import functools

import jax
import jax.numpy as jnp
from jax import lax
from jax.experimental import pallas as pl
from jax.experimental.pallas import tpu as pltpu
from jax.sharding import PartitionSpec as P

MESH = pl.DeviceIdType.MESH
F32 = jnp.float32
BF16 = jnp.bfloat16
BLK = 128
W = 256
XR = 64
YR = BLK - XR
NSTEP = 8
SLOT = {"2o": 0, "2w": 1, "1o": 2, "3o": 3, "1w": 4, "3w": 5, "0o": 6, "0w": 7}

CORE = 0
NEAR = CORE + 8
LEG1 = NEAR + 1
LEG2 = LEG1 + 4
YLEG = LEG2 + 2
YF = YLEG + 1
YLEG1 = YF + 4
YLEG2 = YLEG1 + 2
GC = YLEG2 + 1
R1 = GC + 3
R2 = R1 + 3
R3 = R2 + 3
GF = R3 + 3
NSEM = GF + 3
ROUNDS = 3


def split(a):
    hi = a.astype(BF16)
    return hi, (a - hi.astype(F32)).astype(BF16)


def dot3(a, b):
    d = functools.partial(jnp.dot, preferred_element_type=F32)
    (ah, al), (bh, bl) = a, b
    return d(ah, bh) + d(al, bh) + d(ah, bl)


def join(parts, axis):
    return tuple(jnp.concatenate(p, axis=axis) for p in zip(*parts))


def kernel(
    inv_ref, pat_ref, f1_ref, f2_ref, rows1_ref, rows2_ref, coup_ref, d1_ref, d2_ref,
    p1_out, p2_out, b1_out, bc_out, b2_out,
    a, fac, xh, xl, own, give, got, near, nt, nn, l1, r2, ry, yf, yl1, yr2,
    g, gc, r1, zs, res, const, pan, csp,
    ssem, rsem, lsem, asem, round_sem,
):
    row, col = lax.axis_index("row"), lax.axis_index("col")
    core = lax.rem(col, 2)
    y_lo, z, yh = row // 4, lax.rem(row, 4), lax.rem(col // 2, 2)
    pos = {"x": col // 4, "y": yh * 2 + y_lo, "z": z}
    other = 1 - core

    def device(x, y, z, c):
        return (lax.rem(y, 2) * 4 + z, x * 4 + (y // 2) * 2 + c)

    def at(x=0, y=0, z=0, flip=False):
        return device(
            lax.rem(pos["x"] + x, 4), lax.rem(pos["y"] + y, 4), lax.rem(pos["z"] + z, 4),
            other if flip else core,
        )

    def send(src, dst, k, dev):
        pltpu.make_async_remote_copy(
            src, dst, ssem.at[k], rsem.at[k], device_id=dev, device_id_type=MESH
        ).start()

    me = at()

    def arrived(dst, k):
        pltpu.make_async_remote_copy(
            dst, dst, ssem.at[k], rsem.at[k], device_id=me, device_id_type=MESH
        ).wait_recv()

    def sent(src, k):
        pltpu.make_async_remote_copy(
            src, src, ssem.at[k], rsem.at[k], device_id=me, device_id_type=MESH
        ).wait_send()

    neighbours = [at(x=1), at(x=3), at(y=1), at(y=3), at(z=1), at(z=3)]
    x_up, x_down, y_two, mate = at(x=1), at(x=3), at(y=2), at(flip=True)

    barrier = pltpu.get_barrier_semaphore()
    for dev in [*neighbours, y_two, mate]:
        pl.semaphore_signal(barrier, inc=1, device_id=dev, device_id_type=MESH)

    loads = [
        pltpu.make_async_copy(f1_ref, fac.at[0], lsem.at[0]),
        pltpu.make_async_copy(f2_ref, fac.at[1], lsem.at[1]),
    ]
    for copy in loads:
        copy.start()

    def place(s):
        dx = jnp.where(s < 2, 2, jnp.where(s > 5, 0, 1 + 2 * lax.rem(s, 2)))
        same = jnp.where((s == 1) | (s == 4) | (s == 5) | (s == 7), 1, 0)
        return lax.rem(pos["x"] + dx, 4) * 2 + lax.rem(yh + 1 + same, 2)

    def load_a(s):
        return pltpu.make_async_copy(
            inv_ref.at[pl.ds(pl.multiple_of(place(s) * 256, 256), 256)], a.at[s], asem.at[s]
        )

    for s in range(NSTEP):
        load_a(s).start()
    small = [
        pltpu.make_async_copy(coup_ref, csp, lsem.at[2]),
        pltpu.make_async_copy(d1_ref, const.at[0], lsem.at[3]),
        pltpu.make_async_copy(d2_ref, const.at[2], lsem.at[4]),
    ]
    for copy in small:
        copy.start()

    def member(rows_ref, first, count):
        ids = lax.broadcasted_iota(jnp.int32, (8, 64), 0) + first
        hits = (ids == rows_ref[...].reshape(1, 64)).astype(F32)
        return jnp.sum(hits, axis=1, keepdims=True)[:count]

    for p, rows_ref in enumerate((rows1_ref, rows2_ref)):
        keep = member(rows_ref, col * 8, 8)
        loads[p].wait()
        for j in range(8):
            rows = slice(j * BLK, (j + 1) * BLK)
            hi, lo = split(fac[p, rows, :] * keep[j : j + 1, :])
            xh[rows, p * W : (p + 1) * W] = hi
            xl[rows, p * W : (p + 1) * W] = lo

    to_ylo = pos["x"] // 2
    to_z = 2 * lax.rem(pos["x"], 2) + yh
    to_x = lax.rem(pos["x"] + 2 + to_z + 4 - z, 4)
    to_yh = jnp.where(to_ylo == y_lo, yh, 1 - yh)
    serves = core == to_x // 2

    def send_near():
        @pl.when(serves)
        def _():
            for c in range(2):
                block = lax.rem(to_x, 2) * 4 + to_yh * 2 + c
                rows = pl.ds(pl.multiple_of(block * BLK, BLK), BLK)
                send(fac.at[:, rows], near, NEAR, device(to_x, to_yh * 2 + to_ylo, to_z, c))

    def compute(s):
        load_a(s).wait()
        base = place(s) * 2
        parts = []
        for half in (other, core):
            r0 = pl.multiple_of(half * BLK, BLK)
            parts.append(
                jnp.concatenate(
                    [
                        a[s, pl.ds(r0, BLK), j * BLK : (j + 1) * BLK]
                        * pat_ref[j, base + half].astype(F32)
                        for j in range(8)
                    ],
                    axis=1,
                )
            )
        out = dot3(split(jnp.concatenate(parts, axis=0)), (xh[...], xl[...]))
        for p in range(2):
            give[s, p] = out[:BLK, p * W : (p + 1) * W]
            own[s, p] = out[BLK:, p * W : (p + 1) * W]

    lo_rows, hi_rows = pl.ds(0, XR), pl.ds(XR, YR)

    def fold(s):
        arrived(got.at[s], CORE + s)
        own[s] += got[s]

    def leg1(w, s):
        send(own.at[s, 0, lo_rows], l1.at[w, 0], LEG1 + 2 * w, x_up)
        send(own.at[s, 1, lo_rows], l1.at[w, 1], LEG1 + 2 * w + 1, x_down)

    def leg2_up(w, s):
        send(own.at[s, 1, lo_rows], r2.at[w, 0, 1], LEG2 + w, x_up)

    def leg2_down(w, s):
        send(own.at[s, 0, lo_rows], r2.at[w, 1, 0], LEG2 + w, x_down)

    def relay(w, up, down):
        for d, s, dev in ((0, up, x_up), (1, down, x_down)):
            arrived(l1.at[w, d], LEG1 + 2 * w + d)
            own[s, d, :XR] += l1[w, d]
            send(own.at[s, d, lo_rows], r2.at[w, d, d], LEG2 + w, dev)

    def give_y(dx, s):
        send(own.at[s, :, hi_rows], yf.at[dx], YF + dx, y_two)

    def fold_y(dx, s):
        arrived(yf.at[dx], YF + dx)
        own[s, :, XR:] += yf[dx]

    def hear(k):
        pl.semaphore_wait(round_sem.at[k], 6)

    def tell(k):
        for dev in neighbours:
            pl.semaphore_signal(round_sem.at[k], inc=1, device_id=dev, device_id_type=MESH)

    def after(t):
        if t == 0:
            leg1(0, 0)
            give_y(2, 0)
        elif t == 1:
            leg1(1, 1)
            hear(0)
            tell(1)
        elif t == 2:
            leg2_up(0, 2)
            give_y(1, 2)
        elif t == 3:
            leg2_down(0, 3)
            give_y(3, 3)
            relay(0, 2, 3)
            hear(1)
            tell(2)
        elif t == 4:
            leg2_up(1, 4)
        elif t == 5:
            leg2_down(1, 5)
            hear(2)
            send_near()
            relay(1, 4, 5)
        elif t == 6:
            give_y(0, 6)
            fold_y(2, 1)
            send(own.at[1, 0, hi_rows], yl1.at[0], YLEG1, x_up)
            send(own.at[1, 1, hi_rows], yl1.at[1], YLEG1 + 1, x_down)

    def step(s, carry):
        compute(s)

        @pl.when(s == 0)
        def _():
            pl.semaphore_wait(barrier, 8)
            tell(0)

        send(give.at[s], got.at[s], CORE + s, mate)
        for t in range(NSTEP - 1):

            @pl.when(s == t + 1)
            def _(t=t):
                fold(t)
                after(t)

        return carry

    lax.fori_loop(0, NSTEP, step, 0)
    fold(7)

    arrived(r2.at[0], LEG2)
    own[6, :, :XR] += r2[0, 0] + r2[0, 1]
    send(own.at[6, :, lo_rows], ry, YLEG, y_two)

    def second_leg(d, dx, s, dev):
        fold_y(dx, s)
        send(own.at[s, 1 - d, hi_rows], yr2.at[d, 1 - d], YLEG2, dev)
        arrived(yl1.at[d], YLEG1 + d)
        own[s, d, XR:] += yl1[d]
        send(own.at[s, d, hi_rows], yr2.at[d, d], YLEG2, dev)

    second_leg(0, 1, 4, x_up)

    for copy in small:
        copy.wait()
    coup = csp[...]
    c_split, ct_split = split(coup), split(coup.T)
    d1c = dot3(split(const[0]), c_split)
    const[1] = -d1c
    const[2] += dot3(ct_split, split(d1c))

    second_leg(1, 3, 5, x_down)

    arrived(near, NEAR)
    own_id = row * 16 + col
    n1 = near[0] * member(rows1_ref, own_id, 1)
    n2 = near[1] * member(rows2_ref, own_id, 1)
    n1c = dot3(split(n1), c_split)
    for k, v in enumerate((n1, n2, n1c)):
        nt[0, k], nt[1, k] = split(v.T)
    nn[0], nn[1] = split(n2)

    fold_y(0, 7)
    arrived(r2.at[1], LEG2 + 1)
    own[7, :, :XR] += r2[1, 0] + r2[1, 1]
    arrived(yr2, YLEG2)
    own[7, :, XR:] += yr2[0] + yr2[1]
    arrived(ry, YLEG)
    own[7, :, :XR] += ry[...]

    mine, theirs = pl.multiple_of(core * BLK, BLK), pl.multiple_of(other * BLK, BLK)
    half = pl.ds(mine, BLK)

    def put(m, value):
        g[m] = value
        send(g.at[m, pl.ds(theirs, BLK)], gc.at[m], GC + m, mate)

    m1, m2 = own[7, 0], own[7, 1]
    m1s, m1t = split(m1), split(m1.T)
    n1t, n2t, n1ct = ((nt[0, k], nt[1, k]) for k in range(3))
    n2s = (nn[0], nn[1])
    put(0, dot3(n1t, m1s))
    mc = dot3(m1s, c_split)
    mcs = split(mc)
    minus = lambda v: tuple(-u for u in v)
    put(1, dot3(join((m1t, n1t), 1), join((n2s, minus(mcs)), 0)))
    p2 = mc - m2
    put(2, dot3(join((n2t, split(mc.T), n1ct), 1), join((split(-p2), minus(n2s), mcs), 0)))
    pan[0] = -m1
    pan[1] = p2
    outs = [
        pltpu.make_async_copy(pan.at[0], p1_out, lsem.at[0]),
        pltpu.make_async_copy(pan.at[1], p2_out, lsem.at[1]),
    ]
    for copy in outs:
        copy.start()

    planes = (("x", "y", "z"), ("y", "z", "x"), ("z", "x", "y"))

    def shifted(m, i, j, k):
        return at(**dict(zip(planes[m], (i, j, k))))

    def piece(m, i, j):
        u, v, _ = planes[m]
        index = lax.rem(pos[u] + i, 4) * 4 + lax.rem(pos[v] + j, 4)
        return pl.ds(pl.multiple_of(mine + index * 8, 8), 8)

    order = sorted(
        ((i, j) for i in range(4) for j in range(4) if (i, j) != (0, 0)),
        key=lambda q: -(min(q[0], 4 - q[0]) + min(q[1], 4 - q[1])),
    )
    for m in range(3):
        arrived(gc.at[m], GC + m)
        g[m, half] += gc[m]
        for i, j in order:
            send(g.at[m, piece(m, i, j)], r1.at[m, i * 4 + j], R1 + m, shifted(m, i, j, 0))
    for m in range(3):
        arrived(r1.at[m, 1:16], R1 + m)
        total = g[m, piece(m, 0, 0)]
        for q in range(1, 16):
            total += r1[m, q]
        slot = pos[planes[m][2]]
        zs[m, slot] = total
        for k in (2, 1, 3):
            send(zs.at[m, slot], zs.at[m, slot], R2 + m, shifted(m, 0, 0, k))
    for m in range(3):
        arrived(zs.at[m, 1:4], R2 + m)
        at_piece = piece(m, 0, 0)
        res[m, at_piece] = const[m, at_piece] + ((zs[m, 0] + zs[m, 1]) + (zs[m, 2] + zs[m, 3]))
        for i, j in order:
            send(res.at[m, at_piece], res.at[m, at_piece], R3 + m, shifted(m, i, j, 0))
    for m in range(3):
        arrived(res.at[m, 0:120], R3 + m)
        send(res.at[m, half], res.at[m, half], GF + m, mate)
    for m, out in enumerate((b1_out, bc_out, b2_out)):
        arrived(res.at[m, pl.ds(theirs, BLK)], GF + m)
        outs.append(pltpu.make_async_copy(res.at[m], out, lsem.at[2 + m]))
        outs[-1].start()

    for s in range(NSTEP):
        sent(give.at[s], CORE + s)

    @pl.when(serves)
    def _():
        sent(fac.at[:, 0 : 2 * BLK], NEAR)

    for k in range(4):
        sent(l1.at[0, 0], LEG1 + k)
        sent(yf.at[0], YF + k)
    for k in range(2):
        sent(r2.at[k], LEG2 + k)
        sent(yl1.at[0], YLEG1 + k)
    sent(ry, YLEG)
    sent(yr2, YLEG2)
    for m in range(3):
        sent(gc.at[m], GC + m)
        sent(r1.at[m, 1:16], R1 + m)
        sent(r1.at[m, 1:4], R2 + m)
        sent(r1.at[m, 1:16], R3 + m)
        sent(gc.at[m], GF + m)
    for copy in outs:
        copy.wait()


def per_device(inverse, pattern, first, second, rows1, rows2, coupling, diag1, diag2):
    any_, vmem, smem = (
        pl.BlockSpec(memory_space=pl.ANY),
        pl.BlockSpec(memory_space=pltpu.VMEM),
        pl.BlockSpec(memory_space=pltpu.SMEM),
    )
    V = pltpu.VMEM
    outs = pl.pallas_call(
        kernel,
        out_shape=[jax.ShapeDtypeStruct((BLK, W), F32)] * 2 + [jax.ShapeDtypeStruct((W, W), F32)] * 3,
        in_specs=[any_, smem, any_, any_, vmem, vmem, any_, any_, any_],
        out_specs=[any_] * 5,
        scratch_shapes=[
            V((8, 256, 1024), F32),
            V((2, 1024, W), F32),
            V((1024, 2 * W), BF16),
            V((1024, 2 * W), BF16),
            V((8, 2, BLK, W), F32),
            V((8, 2, BLK, W), F32),
            V((8, 2, BLK, W), F32),
            V((2, BLK, W), F32),
            V((2, 3, W, BLK), BF16),
            V((2, BLK, W), BF16),
            V((2, 2, XR, W), F32),
            V((2, 2, 2, XR, W), F32),
            V((2, XR, W), F32),
            V((4, 2, YR, W), F32),
            V((2, YR, W), F32),
            V((2, 2, YR, W), F32),
            V((3, W, W), F32),
            V((3, BLK, W), F32),
            V((3, 16, 8, W), F32),
            V((3, 4, 8, W), F32),
            V((3, W, W), F32),
            V((3, W, W), F32),
            V((2, BLK, W), F32),
            V((W, W), F32),
            pltpu.SemaphoreType.DMA((NSEM,)),
            pltpu.SemaphoreType.DMA((NSEM,)),
            pltpu.SemaphoreType.DMA((5,)),
            pltpu.SemaphoreType.DMA((8,)),
            pltpu.SemaphoreType.REGULAR((ROUNDS,)),
        ],
        compiler_params=pltpu.CompilerParams(
            collective_id=0, has_side_effects=True, vmem_limit_bytes=62 * 2**20
        ),
    )(inverse, pattern.T, first, second, rows1, rows2, coupling, diag1, diag2)
    return pl.pallas_call(
        hand_over,
        out_shape=[jax.ShapeDtypeStruct(o.shape, o.dtype) for o in outs],
        in_specs=[vmem] * 5,
        out_specs=[any_] * 5,
        scratch_shapes=[pltpu.SemaphoreType.DMA((5,))],
    )(*outs)


def hand_over(*refs):
    sem = refs[-1]
    copies = [pltpu.make_async_copy(refs[i], refs[5 + i], sem.at[i]) for i in range(5)]
    for copy in copies:
        copy.start()
    for copy in copies:
        copy.wait()


def solution(mesh):
    return jax.shard_map(
        per_device,
        mesh=mesh,
        in_specs=(
            P("row", "col"), P("row", "col"), P("col", None), P("col", None),
            P(), P(), P(), P(), P(),
        ),
        out_specs=(P(("row", "col"), None), P(("row", "col"), None), P(), P(), P()),
        check_vma=False,
    )
```

time: 68 us -> 58.5 us (0.86)
  local copies, waits for them, and re-layouts: 9.5 us -> 0 us
    unnamed x6 -> x0, local copies, waits for them, and re-layouts: 9.5 us -> none
    pallas_call x0 -> x1, Pallas kernels: none -> 2.25 us  [per_device(): pl.pallas_call(hand_over, out_shape=[jax.ShapeDtypeStruct(o.shape, o.dtyp...]
    pallas_call x1, Pallas kernels: 57.6 us -> 55.4 us  [per_device(): pl.pallas_call(kernel, out_shape=[jax.ShapeDtypeStruct((BLK, W), F32)] *...]
where the time goes in v2:
time: 58.5 us; the launch traced here: 58.3 us
  Pallas kernels  57.7 us (99%)
  between operations  0.64 us (1%)
    pallas_call x1, Pallas kernels, per_device(): pl.pallas_call(kernel, out_shape=[jax.ShapeDtypeStruct((BLK, W), F32)] *...  55.4 us
    pallas_call x1, Pallas kernels, per_device(): pl.pallas_call(hand_over, out_shape=[jax.ShapeDtypeStruct(o.shape, o.dtyp...  2.25 us

profile of v2, /device:TPU:1, one launch (start us, length us, event | category | flops | bytes accessed | tf_op | source)
XLA Modules:
  0.0 58.3 jit_solution(5379893691300007651)
XLA Ops:
  0.6 55.4 %shard_map.128 = (f32[128,256]{1,0:T(8,128)}, f32[128,256]{1,0:T(8,128)}, f32[256,256]{1,0:T(8,128)}, f32[256,256]{1,0:T(8,128)}, f32[256,256]{1,0:T(8,128)}) custom-call(f32[2048,1024]{1,0:T(8,128)} %inv_ref.1, s32[8,16]{1,0:T(8,128)} %bitcast.1, f32[1024,256]{1,0:T(8,128)} %f1_ref.1, f32[1024,256]{1,0:T(8,128)} %f2_ref.1, s32[64]{0:T(128)} %rows1_ref.1, ...), custom_call_target="tpu_custom_call" | custom-call | tf_op jit(solution)/shard_map/pallas_call | solution.py:402
  56.1 2.2 %shard_map.129 = (f32[128,256]{1,0:T(8,128)}, f32[128,256]{1,0:T(8,128)}, f32[256,256]{1,0:T(8,128)}, f32[256,256]{1,0:T(8,128)}, f32[256,256]{1,0:T(8,128)}) custom-call(f32[128,256]{1,0:T(8,128)} %get-tuple-element.10.refs_0_, f32[128,256]{1,0:T(8,128)} %get-tuple-element.11.refs_1_, f32[256,256]{1,0:T(8,128)} %get-tuple-element.12.refs_2_, ...), custom_call_target="tpu_custom_call" | custom-call | tf_op jit(solution)/shard_map/pallas_call | solution.py:442

commit v3 on v2

--- a/solution.py
+++ b/solution.py
@@ -50,12 +50,24 @@
 
 
 def kernel(
-    inv_ref, pat_ref, f1_ref, f2_ref, rows1_ref, rows2_ref, coup_ref, d1_ref, d2_ref,
+    inv_ref, pat_hbm, f1_ref, f2_ref, rows1_hbm, rows2_hbm, coup_ref, d1_ref, d2_ref,
     p1_out, p2_out, b1_out, bc_out, b2_out,
     a, fac, xh, xl, own, give, got, near, nt, nn, l1, r2, ry, yf, yl1, yr2,
-    g, gc, r1, zs, res, const, pan, csp,
+    g, gc, r1, zs, res, const, csp, rows1_ref, rows2_ref, pat_ref,
     ssem, rsem, lsem, asem, round_sem,
 ):
+    loads = [
+        pltpu.make_async_copy(f1_ref, fac.at[0], lsem.at[0]),
+        pltpu.make_async_copy(f2_ref, fac.at[1], lsem.at[1]),
+    ]
+    tiny = [
+        pltpu.make_async_copy(rows1_hbm, rows1_ref, lsem.at[5]),
+        pltpu.make_async_copy(rows2_hbm, rows2_ref, lsem.at[6]),
+        pltpu.make_async_copy(pat_hbm, pat_ref, lsem.at[7]),
+    ]
+    for copy in tiny + loads:
+        copy.start()
+
     row, col = lax.axis_index("row"), lax.axis_index("col")
     core = lax.rem(col, 2)
     y_lo, z, yh = row // 4, lax.rem(row, 4), lax.rem(col // 2, 2)
@@ -91,16 +103,20 @@
     neighbours = [at(x=1), at(x=3), at(y=1), at(y=3), at(z=1), at(z=3)]
     x_up, x_down, y_two, mate = at(x=1), at(x=3), at(y=2), at(flip=True)
 
+    home = 2 * y_lo + z // 2
+    from_ylo = jnp.where(lax.rem(z, 2) == yh, y_lo, 1 - y_lo)
+    from_z = lax.rem(z + pos["x"] - home + 7 - 2 * core, 4)
+    near_dev = device(home, lax.rem(z, 2) * 2 + from_ylo, from_z, pos["x"] // 2)
+    to_ylo = pos["x"] // 2
+    to_z = 2 * lax.rem(pos["x"], 2) + yh
+    to_yh = jnp.where(to_ylo == y_lo, yh, 1 - yh)
+    to_x0 = lax.rem(pos["x"] + z - to_z + 5, 4)
+    to_core = jnp.where(core == to_x0 // 2, 0, 1)
+    to_x = lax.rem(to_x0 + 2 * to_core, 4)
+
     barrier = pltpu.get_barrier_semaphore()
-    for dev in [*neighbours, y_two, mate]:
+    for dev in [*neighbours, y_two, mate, near_dev]:
         pl.semaphore_signal(barrier, inc=1, device_id=dev, device_id_type=MESH)
-
-    loads = [
-        pltpu.make_async_copy(f1_ref, fac.at[0], lsem.at[0]),
-        pltpu.make_async_copy(f2_ref, fac.at[1], lsem.at[1]),
-    ]
-    for copy in loads:
-        copy.start()
 
     def place(s):
         dx = jnp.where(s < 2, 2, jnp.where(s > 5, 0, 1 + 2 * lax.rem(s, 2)))
@@ -112,21 +128,21 @@
             inv_ref.at[pl.ds(pl.multiple_of(place(s) * 256, 256), 256)], a.at[s], asem.at[s]
         )
 
-    for s in range(NSTEP):
+    for s in range(2):
         load_a(s).start()
     small = [
         pltpu.make_async_copy(coup_ref, csp, lsem.at[2]),
         pltpu.make_async_copy(d1_ref, const.at[0], lsem.at[3]),
         pltpu.make_async_copy(d2_ref, const.at[2], lsem.at[4]),
     ]
-    for copy in small:
-        copy.start()
 
     def member(rows_ref, first, count):
         ids = lax.broadcasted_iota(jnp.int32, (8, 64), 0) + first
         hits = (ids == rows_ref[...].reshape(1, 64)).astype(F32)
         return jnp.sum(hits, axis=1, keepdims=True)[:count]
 
+    for copy in tiny:
+        copy.wait()
     for p, rows_ref in enumerate((rows1_ref, rows2_ref)):
         keep = member(rows_ref, col * 8, 8)
         loads[p].wait()
@@ -136,19 +152,15 @@
             xh[rows, p * W : (p + 1) * W] = hi
             xl[rows, p * W : (p + 1) * W] = lo
 
-    to_ylo = pos["x"] // 2
-    to_z = 2 * lax.rem(pos["x"], 2) + yh
-    to_x = lax.rem(pos["x"] + 2 + to_z + 4 - z, 4)
-    to_yh = jnp.where(to_ylo == y_lo, yh, 1 - yh)
-    serves = core == to_x // 2
-
-    def send_near():
-        @pl.when(serves)
-        def _():
-            for c in range(2):
-                block = lax.rem(to_x, 2) * 4 + to_yh * 2 + c
-                rows = pl.ds(pl.multiple_of(block * BLK, BLK), BLK)
-                send(fac.at[:, rows], near, NEAR, device(to_x, to_yh * 2 + to_ylo, to_z, c))
+    for s in range(2, NSTEP):
+        load_a(s).start()
+    for copy in small:
+        copy.start()
+
+    pl.semaphore_wait(barrier, 9)
+    block = lax.rem(to_x, 2) * 4 + to_yh * 2 + to_core
+    served = pl.ds(pl.multiple_of(block * BLK, BLK), BLK)
+    send(fac.at[:, served], near, NEAR, device(to_x, to_yh * 2 + to_ylo, to_z, to_core))
 
     def compute(s):
         load_a(s).wait()
@@ -213,37 +225,29 @@
             give_y(2, 0)
         elif t == 1:
             leg1(1, 1)
-            hear(0)
-            tell(1)
         elif t == 2:
             leg2_up(0, 2)
             give_y(1, 2)
+            hear(0)
+            tell(1)
         elif t == 3:
             leg2_down(0, 3)
             give_y(3, 3)
-            relay(0, 2, 3)
-            hear(1)
-            tell(2)
         elif t == 4:
             leg2_up(1, 4)
         elif t == 5:
             leg2_down(1, 5)
-            hear(2)
-            send_near()
-            relay(1, 4, 5)
+            hear(1)
+            tell(2)
         elif t == 6:
             give_y(0, 6)
+            relay(0, 2, 3)
             fold_y(2, 1)
             send(own.at[1, 0, hi_rows], yl1.at[0], YLEG1, x_up)
             send(own.at[1, 1, hi_rows], yl1.at[1], YLEG1 + 1, x_down)
 
     def step(s, carry):
         compute(s)
-
-        @pl.when(s == 0)
-        def _():
-            pl.semaphore_wait(barrier, 8)
-            tell(0)
 
         send(give.at[s], got.at[s], CORE + s, mate)
         for t in range(NSTEP - 1):
@@ -255,8 +259,10 @@
 
         return carry
 
+    tell(0)
     lax.fori_loop(0, NSTEP, step, 0)
     fold(7)
+    relay(1, 4, 5)
 
     arrived(r2.at[0], LEG2)
     own[6, :, :XR] += r2[0, 0] + r2[0, 1]
@@ -295,6 +301,7 @@
     own[7, :, :XR] += r2[1, 0] + r2[1, 1]
     arrived(yr2, YLEG2)
     own[7, :, XR:] += yr2[0] + yr2[1]
+    hear(2)
     arrived(ry, YLEG)
     own[7, :, :XR] += ry[...]
 
@@ -316,15 +323,8 @@
     put(1, dot3(join((m1t, n1t), 1), join((n2s, minus(mcs)), 0)))
     p2 = mc - m2
     put(2, dot3(join((n2t, split(mc.T), n1ct), 1), join((split(-p2), minus(n2s), mcs), 0)))
-    pan[0] = -m1
-    pan[1] = p2
-    outs = [
-        pltpu.make_async_copy(pan.at[0], p1_out, lsem.at[0]),
-        pltpu.make_async_copy(pan.at[1], p2_out, lsem.at[1]),
-    ]
-    for copy in outs:
-        copy.start()
-
+    p1_out[...] = -m1
+    p2_out[...] = p2
     planes = (("x", "y", "z"), ("y", "z", "x"), ("z", "x", "y"))
 
     def shifted(m, i, j, k):
@@ -364,16 +364,12 @@
         send(res.at[m, half], res.at[m, half], GF + m, mate)
     for m, out in enumerate((b1_out, bc_out, b2_out)):
         arrived(res.at[m, pl.ds(theirs, BLK)], GF + m)
-        outs.append(pltpu.make_async_copy(res.at[m], out, lsem.at[2 + m]))
-        outs[-1].start()
+        out[...] = res[m]
 
     for s in range(NSTEP):
         sent(give.at[s], CORE + s)
 
-    @pl.when(serves)
-    def _():
-        sent(fac.at[:, 0 : 2 * BLK], NEAR)
-
+    sent(near, NEAR)
     for k in range(4):
         sent(l1.at[0, 0], LEG1 + k)
         sent(yf.at[0], YF + k)
@@ -388,22 +384,16 @@
         sent(r1.at[m, 1:4], R2 + m)
         sent(r1.at[m, 1:16], R3 + m)
         sent(gc.at[m], GF + m)
-    for copy in outs:
-        copy.wait()
 
 
 def per_device(inverse, pattern, first, second, rows1, rows2, coupling, diag1, diag2):
-    any_, vmem, smem = (
-        pl.BlockSpec(memory_space=pl.ANY),
-        pl.BlockSpec(memory_space=pltpu.VMEM),
-        pl.BlockSpec(memory_space=pltpu.SMEM),
-    )
+    any_, vmem = pl.BlockSpec(memory_space=pl.ANY), pl.BlockSpec(memory_space=pltpu.VMEM)
     V = pltpu.VMEM
     outs = pl.pallas_call(
         kernel,
-        out_shape=[jax.ShapeDtypeStruct((BLK, W), F32)] * 2 + [jax.ShapeDtypeStruct((W, W), F32)] * 3,
-        in_specs=[any_, smem, any_, any_, vmem, vmem, any_, any_, any_],
-        out_specs=[any_] * 5,
+        out_shape=[V((BLK, W), F32)] * 2 + [V((W, W), F32)] * 3,
+        in_specs=[pl.BlockSpec(memory_space=pltpu.HBM)] * 9,
+        out_specs=[vmem] * 5,
         scratch_shapes=[
             V((8, 256, 1024), F32),
             V((2, 1024, W), F32),
@@ -427,16 +417,18 @@
             V((3, 4, 8, W), F32),
             V((3, W, W), F32),
             V((3, W, W), F32),
-            V((2, BLK, W), F32),
             V((W, W), F32),
+            V((64,), jnp.int32),
+            V((64,), jnp.int32),
+            pltpu.SMEM((8, 16), jnp.int32),
             pltpu.SemaphoreType.DMA((NSEM,)),
             pltpu.SemaphoreType.DMA((NSEM,)),
-            pltpu.SemaphoreType.DMA((5,)),
+            pltpu.SemaphoreType.DMA((8,)),
             pltpu.SemaphoreType.DMA((8,)),
             pltpu.SemaphoreType.REGULAR((ROUNDS,)),
         ],
         compiler_params=pltpu.CompilerParams(
-            collective_id=0, has_side_effects=True, vmem_limit_bytes=62 * 2**20
+            collective_id=0, has_side_effects=True, vmem_limit_bytes=60 * 2**20
         ),
     )(inverse, pattern.T, first, second, rows1, rows2, coupling, diag1, diag2)
     return pl.pallas_call(
@@ -445,7 +437,7 @@
         in_specs=[vmem] * 5,
         out_specs=[any_] * 5,
         scratch_shapes=[pltpu.SemaphoreType.DMA((5,))],
-    )(*outs)
+    )(*[pltpu.with_memory_space_constraint(o, pltpu.VMEM) for o in outs])
 
 
 def hand_over(*refs):

time: 58.5 us -> 49.1 us (0.84)
  Pallas kernels: 57.7 us -> 48.4 us
    pallas_call x1, Pallas kernels: 55.4 us -> 47.4 us  [per_device(): pl.pallas_call(kernel, out_shape=[V((BLK, W), F32)] * 2 + [V((W, W), F32)...]
    pallas_call x1, Pallas kernels: 2.25 us -> 1.01 us  [per_device(): pl.pallas_call(hand_over, out_shape=[jax.ShapeDtypeStruct(o.shape, o.dtyp...]
where the time goes in v3:
time: 49.1 us; the launch traced here: 49 us
  Pallas kernels  48.4 us (99%)
  between operations  0.64 us (1%)
    pallas_call x1, Pallas kernels, per_device(): pl.pallas_call(kernel, out_shape=[V((BLK, W), F32)] * 2 + [V((W, W), F32)...  47.4 us
    pallas_call x1, Pallas kernels, per_device(): pl.pallas_call(hand_over, out_shape=[jax.ShapeDtypeStruct(o.shape, o.dtyp...  1.01 us

profile of v3, /device:TPU:1, one launch (start us, length us, event | category | flops | bytes accessed | tf_op | source)
XLA Modules:
  0.0 49.0 jit_solution(12759487673393739834)
XLA Ops:
  0.6 47.4 %shard_map.128 = (f32[128,256]{1,0:T(8,128)S(1)}, f32[128,256]{1,0:T(8,128)S(1)}, f32[256,256]{1,0:T(8,128)S(1)}, f32[256,256]{1,0:T(8,128)S(1)}, f32[256,256]{1,0:T(8,128)S(1)}) custom-call(f32[2048,1024]{1,0:T(8,128)} %inv_ref.1, s32[8,16]{1,0:T(8,128)} %bitcast.1, f32[1024,256]{1,0:T(8,128)} %f1_ref.1, f32[1024,256]{1,0:T(8,128)} %f2_ref.1, s32[64]{0:T(128)} %rows1_hbm.1, ...), custom_call_target="tpu_custom_call" | custom-call | tf_op jit(solution)/shard_map/pallas_call | solution.py:392
  48.0 1.0 %shard_map.129 = (f32[128,256]{1,0:T(8,128)}, f32[128,256]{1,0:T(8,128)}, f32[256,256]{1,0:T(8,128)}, f32[256,256]{1,0:T(8,128)}, f32[256,256]{1,0:T(8,128)}) custom-call(f32[128,256]{1,0:T(8,128)S(1)} %get-tuple-element.10.refs_0_, f32[128,256]{1,0:T(8,128)S(1)} %get-tuple-element.11.refs_1_, f32[256,256]{1,0:T(8,128)S(1)} %get-tuple-element.12.refs_2_, ...), custom_call_target="tpu_custom_call" | custom-call | tf_op jit(solution)/shard_map/pallas_call | solution.py:434

commit v4 on v3

--- a/solution.py
+++ b/solution.py
@@ -12,7 +12,7 @@
 BF16 = jnp.bfloat16
 BLK = 128
 W = 256
-XR = 64
+XR = 72
 YR = BLK - XR
 NSTEP = 8
 SLOT = {"2o": 0, "2w": 1, "1o": 2, "3o": 3, "1w": 4, "3w": 5, "0o": 6, "0w": 7}
@@ -83,21 +83,21 @@
             other if flip else core,
         )
 
-    def send(src, dst, k, dev):
+    def send(src, dst, k, dev, group=1):
         pltpu.make_async_remote_copy(
-            src, dst, ssem.at[k], rsem.at[k], device_id=dev, device_id_type=MESH
+            src, dst, ssem.at[group], rsem.at[k], device_id=dev, device_id_type=MESH
         ).start()
 
     me = at()
 
     def arrived(dst, k):
         pltpu.make_async_remote_copy(
-            dst, dst, ssem.at[k], rsem.at[k], device_id=me, device_id_type=MESH
+            dst, dst, ssem.at[0], rsem.at[k], device_id=me, device_id_type=MESH
         ).wait_recv()
 
-    def sent(src, k):
+    def sent(like, group):
         pltpu.make_async_remote_copy(
-            src, src, ssem.at[k], rsem.at[k], device_id=me, device_id_type=MESH
+            like, like, ssem.at[group], rsem.at[0], device_id=me, device_id_type=MESH
         ).wait_send()
 
     neighbours = [at(x=1), at(x=3), at(y=1), at(y=3), at(z=1), at(z=3)]
@@ -235,21 +235,22 @@
             give_y(3, 3)
         elif t == 4:
             leg2_up(1, 4)
+            relay(0, 2, 3)
         elif t == 5:
             leg2_down(1, 5)
             hear(1)
             tell(2)
         elif t == 6:
             give_y(0, 6)
-            relay(0, 2, 3)
             fold_y(2, 1)
             send(own.at[1, 0, hi_rows], yl1.at[0], YLEG1, x_up)
             send(own.at[1, 1, hi_rows], yl1.at[1], YLEG1 + 1, x_down)
+            relay(1, 4, 5)
 
     def step(s, carry):
         compute(s)
 
-        send(give.at[s], got.at[s], CORE + s, mate)
+        send(give.at[s], got.at[s], CORE + s, mate, 0)
         for t in range(NSTEP - 1):
 
             @pl.when(s == t + 1)
@@ -262,20 +263,20 @@
     tell(0)
     lax.fori_loop(0, NSTEP, step, 0)
     fold(7)
-    relay(1, 4, 5)
+
+    fold_y(1, 4)
+    send(own.at[4, 1, hi_rows], yr2.at[0, 1], YLEG2, x_up)
 
     arrived(r2.at[0], LEG2)
     own[6, :, :XR] += r2[0, 0] + r2[0, 1]
     send(own.at[6, :, lo_rows], ry, YLEG, y_two)
 
-    def second_leg(d, dx, s, dev):
-        fold_y(dx, s)
-        send(own.at[s, 1 - d, hi_rows], yr2.at[d, 1 - d], YLEG2, dev)
+    fold_y(3, 5)
+    send(own.at[5, 0, hi_rows], yr2.at[1, 0], YLEG2, x_down)
+    for d, s, dev in ((0, 4, x_up), (1, 5, x_down)):
         arrived(yl1.at[d], YLEG1 + d)
         own[s, d, XR:] += yl1[d]
         send(own.at[s, d, hi_rows], yr2.at[d, d], YLEG2, dev)
-
-    second_leg(0, 1, 4, x_up)
 
     for copy in small:
         copy.wait()
@@ -284,8 +285,6 @@
     d1c = dot3(split(const[0]), c_split)
     const[1] = -d1c
     const[2] += dot3(ct_split, split(d1c))
-
-    second_leg(1, 3, 5, x_down)
 
     arrived(near, NEAR)
     own_id = row * 16 + col
@@ -343,7 +342,7 @@
         arrived(gc.at[m], GC + m)
         g[m, half] += gc[m]
         for i, j in order:
-            send(g.at[m, piece(m, i, j)], r1.at[m, i * 4 + j], R1 + m, shifted(m, i, j, 0))
+            send(g.at[m, piece(m, i, j)], r1.at[m, i * 4 + j], R1 + m, shifted(m, i, j, 0), 2)
     for m in range(3):
         arrived(r1.at[m, 1:16], R1 + m)
         total = g[m, piece(m, 0, 0)]
@@ -352,13 +351,13 @@
         slot = pos[planes[m][2]]
         zs[m, slot] = total
         for k in (2, 1, 3):
-            send(zs.at[m, slot], zs.at[m, slot], R2 + m, shifted(m, 0, 0, k))
+            send(zs.at[m, slot], zs.at[m, slot], R2 + m, shifted(m, 0, 0, k), 2)
     for m in range(3):
         arrived(zs.at[m, 1:4], R2 + m)
         at_piece = piece(m, 0, 0)
         res[m, at_piece] = const[m, at_piece] + ((zs[m, 0] + zs[m, 1]) + (zs[m, 2] + zs[m, 3]))
         for i, j in order:
-            send(res.at[m, at_piece], res.at[m, at_piece], R3 + m, shifted(m, i, j, 0))
+            send(res.at[m, at_piece], res.at[m, at_piece], R3 + m, shifted(m, i, j, 0), 2)
     for m in range(3):
         arrived(res.at[m, 0:120], R3 + m)
         send(res.at[m, half], res.at[m, half], GF + m, mate)
@@ -366,24 +365,10 @@
         arrived(res.at[m, pl.ds(theirs, BLK)], GF + m)
         out[...] = res[m]
 
-    for s in range(NSTEP):
-        sent(give.at[s], CORE + s)
-
-    sent(near, NEAR)
-    for k in range(4):
-        sent(l1.at[0, 0], LEG1 + k)
-        sent(yf.at[0], YF + k)
-    for k in range(2):
-        sent(r2.at[k], LEG2 + k)
-        sent(yl1.at[0], YLEG1 + k)
-    sent(ry, YLEG)
-    sent(yr2, YLEG2)
-    for m in range(3):
-        sent(gc.at[m], GC + m)
-        sent(r1.at[m, 1:16], R1 + m)
-        sent(r1.at[m, 1:4], R2 + m)
-        sent(r1.at[m, 1:16], R3 + m)
-        sent(gc.at[m], GF + m)
+    sent(give, 0)
+    rows = 2 * BLK + 12 * XR + 2 * XR + 14 * YR + 6 * BLK
+    sent(a.at[0:4, 0 : rows // 16], 1)
+    sent(fac.at[0, 0 : 3 * (120 + 24 + 120)], 2)
 
 
 def per_device(inverse, pattern, first, second, rows1, rows2, coupling, diag1, diag2):
@@ -421,7 +406,7 @@
             V((64,), jnp.int32),
             V((64,), jnp.int32),
             pltpu.SMEM((8, 16), jnp.int32),
-            pltpu.SemaphoreType.DMA((NSEM,)),
+            pltpu.SemaphoreType.DMA((3,)),
             pltpu.SemaphoreType.DMA((NSEM,)),
             pltpu.SemaphoreType.DMA((8,)),
             pltpu.SemaphoreType.DMA((8,)),

time: 49.1 us -> 47.9 us (0.976)
  Pallas kernels: 48.4 us -> 47.2 us
    pallas_call x1, Pallas kernels: 47.4 us -> 46.2 us  [per_device(): pl.pallas_call(kernel, out_shape=[V((BLK, W), F32)] * 2 + [V((W, W), F32)...]
where the time goes in v4:
time: 47.9 us; the launch traced here: 47.8 us
  Pallas kernels  47.2 us (99%)
  between operations  0.64 us (1%)
    pallas_call x1, Pallas kernels, per_device(): pl.pallas_call(kernel, out_shape=[V((BLK, W), F32)] * 2 + [V((W, W), F32)...  46.2 us
    pallas_call x1, Pallas kernels, per_device(): pl.pallas_call(hand_over, out_shape=[jax.ShapeDtypeStruct(o.shape, o.dtyp...  1.01 us

profile of v4, /device:TPU:1, one launch (start us, length us, event | category | flops | bytes accessed | tf_op | source)
XLA Modules:
  0.0 47.8 jit_solution(2596500001510734538)
XLA Ops:
  0.6 46.2 %shard_map.128 = (f32[128,256]{1,0:T(8,128)S(1)}, f32[128,256]{1,0:T(8,128)S(1)}, f32[256,256]{1,0:T(8,128)S(1)}, f32[256,256]{1,0:T(8,128)S(1)}, f32[256,256]{1,0:T(8,128)S(1)}) custom-call(f32[2048,1024]{1,0:T(8,128)} %inv_ref.1, s32[8,16]{1,0:T(8,128)} %bitcast.1, f32[1024,256]{1,0:T(8,128)} %f1_ref.1, f32[1024,256]{1,0:T(8,128)} %f2_ref.1, s32[64]{0:T(128)} %rows1_hbm.1, ...), custom_call_target="tpu_custom_call" | custom-call | tf_op jit(solution)/shard_map/pallas_call | solution.py:377
  46.8 1.0 %shard_map.129 = (f32[128,256]{1,0:T(8,128)}, f32[128,256]{1,0:T(8,128)}, f32[256,256]{1,0:T(8,128)}, f32[256,256]{1,0:T(8,128)}, f32[256,256]{1,0:T(8,128)}) custom-call(f32[128,256]{1,0:T(8,128)S(1)} %get-tuple-element.10.refs_0_, f32[128,256]{1,0:T(8,128)S(1)} %get-tuple-element.11.refs_1_, f32[256,256]{1,0:T(8,128)S(1)} %get-tuple-element.12.refs_2_, ...), custom_call_target="tpu_custom_call" | custom-call | tf_op jit(solution)/shard_map/pallas_call | solution.py:419

commit v5 on v4

--- a/solution.py
+++ b/solution.py
@@ -115,7 +115,7 @@
     to_x = lax.rem(to_x0 + 2 * to_core, 4)
 
     barrier = pltpu.get_barrier_semaphore()
-    for dev in [*neighbours, y_two, mate, near_dev]:
+    for dev in [near_dev, *neighbours, y_two, mate]:
         pl.semaphore_signal(barrier, inc=1, device_id=dev, device_id_type=MESH)
 
     def place(s):
@@ -128,8 +128,7 @@
             inv_ref.at[pl.ds(pl.multiple_of(place(s) * 256, 256), 256)], a.at[s], asem.at[s]
         )
 
-    for s in range(2):
-        load_a(s).start()
+    load_a(0).start()
     small = [
         pltpu.make_async_copy(coup_ref, csp, lsem.at[2]),
         pltpu.make_async_copy(d1_ref, const.at[0], lsem.at[3]),
@@ -152,7 +151,7 @@
             xh[rows, p * W : (p + 1) * W] = hi
             xl[rows, p * W : (p + 1) * W] = lo
 
-    for s in range(2, NSTEP):
+    for s in range(1, NSTEP):
         load_a(s).start()
     for copy in small:
         copy.start()
@@ -324,7 +323,7 @@
     put(2, dot3(join((n2t, split(mc.T), n1ct), 1), join((split(-p2), minus(n2s), mcs), 0)))
     p1_out[...] = -m1
     p2_out[...] = p2
-    planes = (("x", "y", "z"), ("y", "z", "x"), ("z", "x", "y"))
+    planes = (("y", "z", "x"), ("z", "x", "y"), ("x", "y", "z"))
 
     def shifted(m, i, j, k):
         return at(**dict(zip(planes[m], (i, j, k))))

time: 47.9 us -> 47.5 us (level)
  no operation moved by 1% of the time
where the time goes in v5:
time: 47.5 us; the launch traced here: 47.4 us
  Pallas kernels  46.8 us (99%)
  between operations  0.64 us (1%)
    pallas_call x1, Pallas kernels, per_device(): pl.pallas_call(kernel, out_shape=[V((BLK, W), F32)] * 2 + [V((W, W), F32)...  45.8 us
    pallas_call x1, Pallas kernels, per_device(): pl.pallas_call(hand_over, out_shape=[jax.ShapeDtypeStruct(o.shape, o.dtyp...  1.01 us

profile of v5, /device:TPU:1, one launch (start us, length us, event | category | flops | bytes accessed | tf_op | source)
XLA Modules:
  0.0 47.4 jit_solution(8338546974081821299)
XLA Ops:
  0.6 45.8 %shard_map.128 = (f32[128,256]{1,0:T(8,128)S(1)}, f32[128,256]{1,0:T(8,128)S(1)}, f32[256,256]{1,0:T(8,128)S(1)}, f32[256,256]{1,0:T(8,128)S(1)}, f32[256,256]{1,0:T(8,128)S(1)}) custom-call(f32[2048,1024]{1,0:T(8,128)} %inv_ref.1, s32[8,16]{1,0:T(8,128)} %bitcast.1, f32[1024,256]{1,0:T(8,128)} %f1_ref.1, f32[1024,256]{1,0:T(8,128)} %f2_ref.1, s32[64]{0:T(128)} %rows1_hbm.1, ...), custom_call_target="tpu_custom_call" | custom-call | tf_op jit(solution)/shard_map/pallas_call | solution.py:376
  46.4 1.0 %shard_map.129 = (f32[128,256]{1,0:T(8,128)}, f32[128,256]{1,0:T(8,128)}, f32[256,256]{1,0:T(8,128)}, f32[256,256]{1,0:T(8,128)}, f32[256,256]{1,0:T(8,128)}) custom-call(f32[128,256]{1,0:T(8,128)S(1)} %get-tuple-element.10.refs_0_, f32[128,256]{1,0:T(8,128)S(1)} %get-tuple-element.11.refs_1_, f32[256,256]{1,0:T(8,128)S(1)} %get-tuple-element.12.refs_2_, ...), custom_call_target="tpu_custom_call" | custom-call | tf_op jit(solution)/shard_map/pallas_call | solution.py:418

commit v6 on v5

--- a/solution.py
+++ b/solution.py
@@ -61,9 +61,9 @@
         pltpu.make_async_copy(f2_ref, fac.at[1], lsem.at[1]),
     ]
     tiny = [
-        pltpu.make_async_copy(rows1_hbm, rows1_ref, lsem.at[5]),
-        pltpu.make_async_copy(rows2_hbm, rows2_ref, lsem.at[6]),
-        pltpu.make_async_copy(pat_hbm, pat_ref, lsem.at[7]),
+        pltpu.make_async_copy(rows1_hbm, rows1_ref, lsem.at[3]),
+        pltpu.make_async_copy(rows2_hbm, rows2_ref, lsem.at[4]),
+        pltpu.make_async_copy(pat_hbm, pat_ref, lsem.at[5]),
     ]
     for copy in tiny + loads:
         copy.start()
@@ -131,8 +131,8 @@
     load_a(0).start()
     small = [
         pltpu.make_async_copy(coup_ref, csp, lsem.at[2]),
-        pltpu.make_async_copy(d1_ref, const.at[0], lsem.at[3]),
-        pltpu.make_async_copy(d2_ref, const.at[2], lsem.at[4]),
+        pltpu.make_async_copy(d1_ref, const.at[0], lsem.at[2]),
+        pltpu.make_async_copy(d2_ref, const.at[2], lsem.at[2]),
     ]
 
     def member(rows_ref, first, count):
@@ -277,8 +277,7 @@
         own[s, d, XR:] += yl1[d]
         send(own.at[s, d, hi_rows], yr2.at[d, d], YLEG2, dev)
 
-    for copy in small:
-        copy.wait()
+    pltpu.make_async_copy(const, const, lsem.at[2]).wait()
     coup = csp[...]
     c_split, ct_split = split(coup), split(coup.T)
     d1c = dot3(split(const[0]), c_split)
@@ -335,7 +334,7 @@
 
     order = sorted(
         ((i, j) for i in range(4) for j in range(4) if (i, j) != (0, 0)),
-        key=lambda q: -(min(q[0], 4 - q[0]) + min(q[1], 4 - q[1])),
+        key=lambda q: -(1.01 * min(q[0], 4 - q[0]) + min(q[1], 4 - q[1])),
     )
     for m in range(3):
         arrived(gc.at[m], GC + m)
@@ -407,7 +406,7 @@
             pltpu.SMEM((8, 16), jnp.int32),
             pltpu.SemaphoreType.DMA((3,)),
             pltpu.SemaphoreType.DMA((NSEM,)),
-            pltpu.SemaphoreType.DMA((8,)),
+            pltpu.SemaphoreType.DMA((6,)),
             pltpu.SemaphoreType.DMA((8,)),
             pltpu.SemaphoreType.REGULAR((ROUNDS,)),
         ],

time: 47.5 us -> 47.4 us (level)
  no operation moved by 1% of the time
where the time goes in v6:
time: 47.4 us; the launch traced here: 47.3 us
  Pallas kernels  46.7 us (99%)
  between operations  0.64 us (1%)
    pallas_call x1, Pallas kernels, per_device(): pl.pallas_call(kernel, out_shape=[V((BLK, W), F32)] * 2 + [V((W, W), F32)...  45.7 us
    pallas_call x1, Pallas kernels, per_device(): pl.pallas_call(hand_over, out_shape=[jax.ShapeDtypeStruct(o.shape, o.dtyp...  1.01 us

profile of v6, /device:TPU:1, one launch (start us, length us, event | category | flops | bytes accessed | tf_op | source)
XLA Modules:
  0.0 47.3 jit_solution(883986366378714294)
XLA Ops:
  0.6 45.7 %shard_map.128 = (f32[128,256]{1,0:T(8,128)S(1)}, f32[128,256]{1,0:T(8,128)S(1)}, f32[256,256]{1,0:T(8,128)S(1)}, f32[256,256]{1,0:T(8,128)S(1)}, f32[256,256]{1,0:T(8,128)S(1)}) custom-call(f32[2048,1024]{1,0:T(8,128)} %inv_ref.1, s32[8,16]{1,0:T(8,128)} %bitcast.1, f32[1024,256]{1,0:T(8,128)} %f1_ref.1, f32[1024,256]{1,0:T(8,128)} %f2_ref.1, s32[64]{0:T(128)} %rows1_hbm.1, ...), custom_call_target="tpu_custom_call" | custom-call | tf_op jit(solution)/shard_map/pallas_call | solution.py:375
  46.3 1.0 %shard_map.129 = (f32[128,256]{1,0:T(8,128)}, f32[128,256]{1,0:T(8,128)}, f32[256,256]{1,0:T(8,128)}, f32[256,256]{1,0:T(8,128)}, f32[256,256]{1,0:T(8,128)}) custom-call(f32[128,256]{1,0:T(8,128)S(1)} %get-tuple-element.10.refs_0_, f32[128,256]{1,0:T(8,128)S(1)} %get-tuple-element.11.refs_1_, f32[256,256]{1,0:T(8,128)S(1)} %get-tuple-element.12.refs_2_, ...), custom_call_target="tpu_custom_call" | custom-call | tf_op jit(solution)/shard_map/pallas_call | solution.py:417

commit v7 on v6

--- a/solution.py
+++ b/solution.py
@@ -425,7 +425,7 @@
 
 def hand_over(*refs):
     sem = refs[-1]
-    copies = [pltpu.make_async_copy(refs[i], refs[5 + i], sem.at[i]) for i in range(5)]
+    copies = [pltpu.make_async_copy(refs[i], refs[5 + i], sem.at[i]) for i in (2, 3, 4, 0, 1)]
     for copy in copies:
         copy.start()
     for copy in copies:

time: 47.4 us -> 47.4 us (level)
  no operation moved by 1% of the time
where the time goes in v7:
time: 47.4 us; the launch traced here: 47.3 us
  Pallas kernels  46.7 us (99%)
  between operations  0.64 us (1%)
    pallas_call x1, Pallas kernels, per_device(): pl.pallas_call(kernel, out_shape=[V((BLK, W), F32)] * 2 + [V((W, W), F32)...  45.7 us
    pallas_call x1, Pallas kernels, per_device(): pl.pallas_call(hand_over, out_shape=[jax.ShapeDtypeStruct(o.shape, o.dtyp...  1 us

profile of v7, /device:TPU:1, one launch (start us, length us, event | category | flops | bytes accessed | tf_op | source)
XLA Modules:
  0.0 47.3 jit_solution(9343296525347916795)
XLA Ops:
  0.6 45.7 %shard_map.128 = (f32[128,256]{1,0:T(8,128)S(1)}, f32[128,256]{1,0:T(8,128)S(1)}, f32[256,256]{1,0:T(8,128)S(1)}, f32[256,256]{1,0:T(8,128)S(1)}, f32[256,256]{1,0:T(8,128)S(1)}) custom-call(f32[2048,1024]{1,0:T(8,128)} %inv_ref.1, s32[8,16]{1,0:T(8,128)} %bitcast.1, f32[1024,256]{1,0:T(8,128)} %f1_ref.1, f32[1024,256]{1,0:T(8,128)} %f2_ref.1, s32[64]{0:T(128)} %rows1_hbm.1, ...), custom_call_target="tpu_custom_call" | custom-call | tf_op jit(solution)/shard_map/pallas_call | solution.py:375
  46.3 1.0 %shard_map.129 = (f32[128,256]{1,0:T(8,128)}, f32[128,256]{1,0:T(8,128)}, f32[256,256]{1,0:T(8,128)}, f32[256,256]{1,0:T(8,128)}, f32[256,256]{1,0:T(8,128)}) custom-call(f32[128,256]{1,0:T(8,128)S(1)} %get-tuple-element.10.refs_0_, f32[128,256]{1,0:T(8,128)S(1)} %get-tuple-element.11.refs_1_, f32[256,256]{1,0:T(8,128)S(1)} %get-tuple-element.12.refs_2_, ...), custom_call_target="tpu_custom_call" | custom-call | tf_op jit(solution)/shard_map/pallas_call | solution.py:417
